TPU v7x, 512 devices: a whole 4x4x16 slice. The times are simulated.
512 devices in a mesh: row: 16 (over z_hi, x), col: 32 (over y, z_lo, core).
Axes of the slice: x: 4, y: 4, z: 16 (z_hi: 4, z_lo: 4; z = z_hi * 4 + z_lo), core: 2. Of those that a mesh axis runs over, the one named last changes fastest.
Arguments:
- points: bfloat16 [32768, 768], P(('row', 'col')), may hold values from -8 to 8
- assign: int32 [32768], P(('row', 'col')), may hold values from 0 to 4095, as said below
Outputs:
- distance: float32 [32768, 4096], P('row', 'col')
Inputs may be any that keep to these rules, and one draw needn't show every extreme that they name: Cluster group of a point is assign // 128. Among the 64 points of one device (aligned blocks of 64) at most 4 fall in one cluster group, and in every such block some group has exactly 4.
All inputs are finite; a program needn't handle non-finite values.
Results may differ from a plain program's by a relative error of at most 0.0003.
Values may be sent and summed in bfloat16 or wider, within the bound.
A program may use at most 64 MiB of HBM per device.

v0:
```python
import jax
import jax.numpy as jnp
from jax import lax
from jax.sharding import PartitionSpec as P

D = 768
CL_DEV = 128


def squares(values):
    return jnp.sum(jnp.square(values.astype(jnp.float32)), axis=1)


def kernel_tile(left_rows, left_norms, right_rows, right_norms):
    inner_prod = lax.dot_general(
        left_rows, right_rows, (((1,), (1,)), ((), ())), preferred_element_type=jnp.float32
    )
    squared = left_norms[:, None] + right_norms[None, :] - 2.0 * inner_prod
    return jnp.exp(-squared / D).astype(jnp.bfloat16)


def onehot(slot_ids, cluster_cols):
    return (slot_ids[:, None] == jnp.arange(cluster_cols, dtype=jnp.int32)[None, :]).astype(
        jnp.bfloat16
    )


def per_device(points, assign):
    own_count = points.shape[0]
    group_count = lax.axis_size("col")
    slot_cap = max(2, 2 * own_count // group_count)
    group_of = assign // CL_DEV
    local_ids = assign - group_of * CL_DEV
    member = (group_of[:, None] == jnp.arange(group_count, dtype=jnp.int32)[None, :]).astype(
        jnp.int32
    )
    before = jnp.cumsum(member, axis=0) - member
    position = jnp.sum(before * member, axis=1)
    target = group_of * slot_cap + position
    matches = target[None, :] == jnp.arange(group_count * slot_cap, dtype=jnp.int32)[:, None]
    dispatch = matches.astype(jnp.bfloat16)
    buckets = jnp.dot(dispatch, points, preferred_element_type=jnp.float32).astype(jnp.bfloat16)
    buckets = buckets.reshape(group_count, slot_cap, D)
    slot_ids = jnp.max(jnp.where(matches, local_ids[None, :], -1), axis=1).reshape(
        group_count, slot_cap
    )
    arrived, arrived_ids = (
        lax.all_to_all(buckets, "col", split_axis=0, concat_axis=0, tiled=True),
        lax.all_to_all(slot_ids, "col", split_axis=0, concat_axis=0, tiled=True),
    )
    slice_pts = arrived.reshape(-1, D)
    slice_ids = arrived_ids.reshape(-1)
    row_block = lax.all_gather(points, "col", axis=0, tiled=True)
    block_rows = row_block.shape[0]
    left_rows = jnp.concatenate([row_block, slice_pts], axis=0)
    left_norms = squares(left_rows)
    part_pts = lax.all_gather(slice_pts, "row", axis=0, tiled=True)
    part_ids = lax.all_gather(slice_ids, "row", axis=0, tiled=True)
    tile_vals = kernel_tile(left_rows, left_norms, part_pts, squares(part_pts))
    indicator = onehot(part_ids, CL_DEV)
    all_sums = jnp.dot(tile_vals, indicator, preferred_element_type=jnp.float32)
    counts = jnp.sum(indicator.astype(jnp.float32), axis=0)
    row_sums = all_sums[:block_rows]
    self_rows = all_sums[block_rows:]
    partial_self = jnp.sum(onehot(slice_ids, CL_DEV).astype(jnp.float32) * self_rows, axis=0)
    self_total = lax.psum(partial_self, "row")
    sizes_floor = jnp.maximum(counts, 1.0)
    return (
        1.0
        - 2.0 * row_sums / sizes_floor[None, :]
        + self_total[None, :] / (sizes_floor * sizes_floor)[None, :]
    )


def solution(mesh):
    return jax.shard_map(
        per_device,
        mesh=mesh,
        in_specs=(P(("row", "col"), None), P(("row", "col"))),
        out_specs=P("row", "col"),
        check_vma=False,
    )
```

profile of v0, /device:TPU:8, one launch (start us, length us, event | category | flops | bytes accessed | tf_op | source)
XLA Modules:
  0.0 273.6 jit_solution(12760304313564935615)
XLA Ops:
  6.5 0.7 all-gather.4.cloned.1.call-update
  7.3 0.7 multiply_subtract_fusion
  8.0 0.1 reduce_window_sum.11
  8.1 0.2 select_reduce_fusion.1
  8.3 1.2 convolution_convert_fusion
  9.6 17.5 %all_to_all.14 = bf16[32,4,768]{2,1,0:T(4,128)(2,1)S(1)} all-to-all(bf16[32,4,768]{2,1,0:T(4,128)(2,1)S(1)} %reshape.27), channel_id=1, replica_groups=mesh['row'=16,'col'=32] {'col'}, dimensions={0} | all-to-all | bytes 393216 | tf_op jit(solution)/shard_map/all_to_all | solution.py:48
  27.2 0.7 reshape.28
  27.9 0.1 select_reduce_fusion
  28.0 0.1 all_to_all.10
  28.1 11.2 %all_to_all.15 = s32[32,1,4]{2,1,0:T(1,128)S(1)} all-to-all(s32[32,1,4]{2,1,0:T(1,128)S(1)} %bitcast.7), channel_id=1, replica_groups=mesh['row'=16,'col'=32] {'col'}, dimensions={0} | all-to-all | bytes 1024 | tf_op jit(solution)/shard_map/all_to_all | solution.py:49
  39.3 0.5 broadcast.31
  39.9 0.6 reduce.5
  40.5 0.1 reshape.30
  40.6 0.1 reshape.29
  40.7 55.5 %all-gather = s32[16,1,128]{2,1,0:T(1,128)S(1)} all-gather(s32[1,1,128]{2,1,0:T(1,128)S(1)} %reshape.30), channel_id=1, replica_groups=mesh['row'=16,'col'=32] {'row'}, dimensions={0}, use_global_device_ids=true | all-gather | bytes 8704 | tf_op jit(solution)/shard_map/all_gather | solution.py:58
  96.2 0.3 convert_reduce_fusion
  96.6 2.1 constant_dynamic-update-slice_fusion.1
  98.7 0.7 multiply_reduce_fusion
  99.4 97.6 %all-gather.6.cloned.1.call-done = bf16[2048,768]{1,0:T(8,128)(2,1)} async-done(((bf16[128,768]{1,0:T(8,128)(2,1)}), bf16[2048,768]{1,0:T(8,128)(2,1)}) %all-gather.6.cloned.1.call-update) | async-done | bytes 3145744 | tf_op jit(solution)/shard_map/all_gather | solution.py:57
  197.0 2.6 multiply_reduce_fusion.1
  199.6 12.8 %fusion = f32[2176,128]{1,0:T(8,128)} fusion(bf16[2176,768]{1,0:T(8,128)(2,1)S(1)} %constant_dynamic-update-slice_fusion, bf16[2048,768]{1,0:T(8,128)(2,1)} %all-gather.6.cloned.1.call-done, f32[2048]{0:T(1024)S(1)} %multiply_reduce_fusion.1, f32[2176]{0:T(1024)S(1)} %multiply_reduce_fusion, s32[2048]{0:T(1024)S(1)} %bitcast.9), kind=kOutput, calls=%fused_computation.1 | convolution fusion | flops 8012955648 | bytes 7627264 | tf_op jit(solution)/shard_map/dot_general | solution.py:61
  212.4 0.9 fusion.10
  213.4 51.0 %psum.7 = f32[128]{0:T(128)S(1)} all-reduce(f32[128]{0:T(128)S(1)} %fusion.10), channel_id=1, replica_groups=mesh['row'=16,'col'=32] {'row'}, use_global_device_ids=true, to_apply=%region_7.8 | all-reduce | flops 128 | bytes 1024 | tf_op jit(solution)/shard_map/psum | solution.py:66
  264.4 2.3 fusion.7
  (11 shorter events, 0.2 us)
Async XLA Ops:
  6.5 90.0 %all-gather.4.cloned.1.call-start = ((), (), s32[]{:S(2)}) async-start(), calls=%async_computation.2 | async-start | bytes 3244032 | tf_op jit(solution)/shard_map/all_gather | solution.py:53
  7.3 189.8 %all-gather.6.cloned.1.call-start = ((), (), s32[]{:S(2)}) async-start(), calls=%async_computation.3 | async-start | bytes 3342336 | tf_op jit(solution)/shard_map/all_gather | solution.py:57
  27.9 70.8 %copy-start = (bf16[128,768]{1,0:T(8,128)(2,1)S(1)}, bf16[128,768]{1,0:T(8,128)(2,1)}, u32[]{:S(2)}) copy-start(bf16[128,768]{1,0:T(8,128)(2,1)} %reshape.28) | copy-start | bytes 589828
Sparse Core Ops, SparseCore 0:
  9.5 70.2 all-gather.3
  82.7 114.2 all-gather.5
where the time goes:
time: 274 us
  blocking collectives  135 us (49%)
  waiting for transfers between devices  98.4 us (36%)
  matrix products  14.1 us (5%)
  between operations  13.5 us (5%)
  other arithmetic  8.66 us (3%)
  local copies, waits for them, and re-layouts  3.71 us (1%)
    all_gather x1, waiting for transfers between devices, per_device(): part_pts = lax.all_gather(slice_pts, 'row', axis=0, tiled=True)  97.6 us
    all_gather x1, blocking collectives, per_device(): part_ids = lax.all_gather(slice_ids, 'row', axis=0, tiled=True)  55.5 us
    psum x1, blocking collectives, per_device(): self_total = lax.psum(partial_self, 'row')  51 us
    all_to_all x1, blocking collectives, per_device(): lax.all_to_all(buckets, 'col', split_axis=0, concat_axis=0, tiled=True)  17.5 us
    dot_general x1, matrix products, per_device(): all_sums = jnp.dot(tile_vals, indicator, preferred_element_type=jnp.float32)  12.8 us
    all_to_all x1, blocking collectives, per_device(): lax.all_to_all(slot_ids, 'col', split_axis=0, concat_axis=0, tiled=True)  11.2 us
  transfers between devices with their start and end apart: 2, of which 1 were waited for; matrix products, arithmetic and copies ran while one was open for 3% of the time, Pallas kernels for 0%

commit v1 on v0

v1 whole, which is shorter than its diff:
```python
import jax
import jax.numpy as jnp
from jax import lax
from jax.experimental import pallas as pl
from jax.experimental.pallas import tpu as pltpu
from jax.sharding import PartitionSpec as P

D = 768
CL = 128
PD = 64
SLOT = 4
NX, NY, NZ, ZL = 4, 4, 16, 4
SETS = 8
ROWS = 2048
RT = 512
MESH = pl.DeviceIdType.MESH
F32 = jnp.float32
BF = jnp.bfloat16


def iota(shape, dim):
    return lax.broadcasted_iota(jnp.int32, shape, dim)


def nt_dot(left, right):
    return lax.dot_general(left, right, (((1,), (1,)), ((), ())), preferred_element_type=F32)


def kernel(p_ref, a_ref, o_ref, zb, zm, seld, selo, gb, yo, ids, rowb, ind, nrow, ncol, nleft,
           self_acc, cnt_acc, zr_sem, zmr_sem, yd_sem, yo_sem, x_sem, xl_sem, id_sem,
           rr_sem, rp_sem, send_sem, rsend_sem):
    r = lax.axis_index("row")
    c = lax.axis_index("col")
    x = lax.rem(r, NX)
    zh = r // NX
    y = c // (2 * ZL)
    zl = lax.rem(c // 2, ZL)
    k = lax.rem(c, 2)
    z = zh * ZL + zl

    def dev(dx, dy, dz, other):
        nx = lax.rem(x + dx, NX)
        ny = lax.rem(y + dy, NY)
        nz = lax.rem(z + dz, NZ)
        nk = 1 - k if other is True else (k if other is False else other)
        return (nz // ZL * NX + nx, (ny * ZL + lax.rem(nz, ZL)) * 2 + nk)

    right, left = dev(0, 0, 1, False), dev(0, 0, NZ - 1, False)
    partner = dev(0, 0, 0, True)
    pending = []
    count = [0]

    def send(src, dst, recv, device):
        sem = send_sem.at[count[0]]
        count[0] += 1
        cp = pltpu.make_async_remote_copy(src, dst, sem, recv, device_id=device, device_id_type=MESH)
        cp.start()
        pending.append(cp)

    def arrived(dst, recv):
        pltpu.make_async_copy(dst, dst, recv).wait()

    yo[...] = jnp.zeros_like(yo)
    barrier = pltpu.get_barrier_semaphore()
    peers = [right, left, partner]
    for dy in (1, 2, 3):
        peers += [dev(0, dy, 0, False), dev(0, dy, 0, True)]
    peers += [dev(dx, 0, 0, False) for dx in (1, 2, 3)]
    for peer in peers:
        pl.semaphore_signal(barrier, inc=1, device_id=peer, device_id_type=MESH)

    arow = a_ref[...]
    diag = iota((PD, PD), 0) == iota((PD, PD), 1)

    def to_col(row):
        return jnp.sum(jnp.where(diag, jnp.broadcast_to(row, (PD, PD)), 0), axis=1, keepdims=True)

    grow = arow // CL
    lrow = arow - grow * CL
    gcol = to_col(grow)
    earlier = (gcol == grow) & (iota((PD, PD), 0) < iota((PD, PD), 1))
    pos = jnp.sum(earlier.astype(jnp.int32), axis=0, keepdims=True)
    target = (grow * SLOT + pos).astype(F32)
    both = jnp.concatenate([target, lrow.astype(F32)], axis=1)
    zm[0, 0] = jnp.broadcast_to(both, (8, 2 * PD)).astype(BF)
    pl.semaphore_wait(barrier, len(peers))

    H = PD // 2

    def blk(s, b):
        return p_ref if (s, b) == (0, 0) else zb.at[s, b]

    def ring(s, b, half, ns, nb, device):
        send(blk(s, b).at[pl.ds(half * H, H)], zb.at[ns, nb, pl.ds(half * H, H)],
             zr_sem.at[ns, nb, half], device)

    def ring_meta(s, b, ns, nb, device):
        send(zm.at[s, b], zm.at[ns, nb], zmr_sem.at[ns, nb], device)

    def row_sends(s, b, m):
        src = blk(s, b)
        at = pl.multiple_of(((y * ZL + m) * 2 + k) * PD, PD)
        dst = rowb.at[pl.ds(at, PD)]
        pltpu.make_async_copy(src, dst, rr_sem.at[0, m]).start()
        pltpu.make_async_remote_copy(src, dst, rsend_sem.at[0, m], rp_sem.at[0, m],
                                     device_id=partner, device_id_type=MESH).start()
        for dy in (1, 2, 3):
            pltpu.make_async_remote_copy(src, dst, rsend_sem.at[dy, m], rr_sem.at[dy, m],
                                         device_id=dev(0, dy, 0, False), device_id_type=MESH).start()

    def row_at(dy, m, core):
        ys = lax.rem(y + NY - dy, NY)
        return rowb.at[pl.ds(pl.multiple_of(((ys * ZL + m) * 2 + core) * PD, PD), PD)]

    for half in (0, 1):
        ring(0, 0, half, 1, 0, right)
        ring(0, 0, half, 0, 1, left)
        if half == 0:
            ring_meta(0, 0, 1, 0, right)
            ring_meta(0, 0, 0, 1, left)

    def ring_step(s):
        for half in (0, 1):
            arrived(zb.at[s, 1, pl.ds(half * H, H)], zr_sem.at[s, 1, half])
            if s < SETS - 1:
                ring(s, 1, half, s + 1, 1, left)
            if s > 0:
                arrived(zb.at[s, 0, pl.ds(half * H, H)], zr_sem.at[s, 0, half])
                if s < SETS - 1:
                    ring(s, 0, half, s + 1, 0, right)
            if half == 0:
                arrived(zm.at[s, 1], zmr_sem.at[s, 1])
                if s < SETS - 1:
                    ring_meta(s, 1, s + 1, 1, left)
                if s > 0:
                    arrived(zm.at[s, 0], zmr_sem.at[s, 0])
                    if s < SETS - 1:
                        ring_meta(s, 0, s + 1, 0, right)

    def select(s):
        q = iota((PD, PD), 0)
        dy, core, b, p = q // 16, q // 8 % 2, q // 4 % 2, q % 4
        want = ((lax.rem(y + dy, NY) * ZL + zl) * 2 + core) * SLOT + p
        data = jnp.zeros((PD, D), F32)
        hot = jnp.zeros((PD, CL), F32)
        for bb in (0, 1):
            meta = zm[s, bb][0:1].astype(F32).astype(jnp.int32)
            trow, lrow_ = meta[:, :PD], meta[:, PD:]
            pick = ((trow == want) & (b == bb)).astype(BF)
            local = (to_col(lrow_) == iota((PD, CL), 1)).astype(BF)
            data += jnp.dot(pick, blk(s, bb)[...], preferred_element_type=F32)
            hot += jnp.dot(pick, local, preferred_element_type=F32)
        seld[s] = data.astype(BF)
        selo[s] = hot.astype(BF)

    def dispatch(s):
        for dy in (1, 3, 2, 0):
            src = ((NY - dy) % NY * 2 + k) * 8
            for core in (0, 1):
                if dy == 0 and core == 1:
                    continue
                at = dy * 16 + core * 8
                if dy == 0:
                    dest = partner
                    off = pl.multiple_of((1 - k) * 8, 8)
                else:
                    dest = dev(0, dy, 0, core)
                    off = at
                to = pl.ds(pl.multiple_of(src, 8), 8)
                send(seld.at[s, pl.ds(off, 8)], gb.at[s, 0, to], yd_sem.at[s], dest)
                send(selo.at[s, pl.ds(off, 8)], yo.at[s, to], yo_sem.at[s], dest)
        off = pl.ds(pl.multiple_of(k * 8, 8), 8)
        pltpu.make_async_copy(seld.at[s, off], gb.at[s, 0, off], yd_sem.at[s]).start()
        pltpu.make_async_copy(selo.at[s, off], yo.at[s, off], yo_sem.at[s]).start()

    def x_step(s):
        arrived(gb.at[s, 0], yd_sem.at[s])
        arrived(yo.at[s, pl.ds(0, PD)], yo_sem.at[s])
        send(gb.at[s, 0], gb.at[s, 3], x_sem.at[s, 0], dev(1, 0, 0, False))
        send(gb.at[s, 0], gb.at[s, 1], x_sem.at[s, 1], dev(3, 0, 0, False))
        number = (iota((8, CL), 1) + 1).astype(F32).astype(BF)
        ids[s, 0] = nt_dot(number, yo[s])
        for dx in (1, 2, 3):
            send(ids.at[s, 0], ids.at[s, NX - dx], id_sem.at[s, dx - 1], dev(dx, 0, 0, False))

    def relay(s):
        arrived(gb.at[s, 3], x_sem.at[s, 0])
        lo, hi = pl.ds(0, H), pl.ds(H, H)
        send(gb.at[s, 3, lo], gb.at[s, 2, lo], xl_sem.at[s, 0], dev(1, 0, 0, False))
        arrived(gb.at[s, 1], x_sem.at[s, 1])
        send(gb.at[s, 1, hi], gb.at[s, 2, hi], xl_sem.at[s, 1], dev(3, 0, 0, False))

    def x_done(s):
        arrived(gb.at[s, 2, pl.ds(0, H)], xl_sem.at[s, 0])
        arrived(gb.at[s, 2, pl.ds(H, H)], xl_sem.at[s, 1])
        for dx in (1, 2, 3):
            arrived(ids.at[s, NX - dx], id_sem.at[s, dx - 1])

    def row_relay():
        for dy in (1, 3, 2):
            for m in range(ZL):
                ref = row_at(dy, m, k)
                arrived(ref, rr_sem.at[dy, m])
                send(ref, ref, rp_sem.at[dy, m], partner)

    def row_done():
        for m in range(ZL):
            arrived(row_at(0, m, k), rr_sem.at[0, m])
            for dy in range(NY):
                arrived(row_at(dy, m, 1 - k), rp_sem.at[dy, m])

    inv = 1.0 / D

    def prepare(s):
        def wide(a, b):
            return a + pltpu.roll(b, PD, 1)
        row = jnp.concatenate([wide(ids[s, 0], ids[s, 1]), wide(ids[s, 2], ids[s, 3])], axis=1)
        hot = (row[0:1].astype(jnp.int32) - 1 == iota((CL, 256), 0)).astype(F32)
        ind[s] = hot.T.astype(BF)
        cnt_acc[...] += jnp.broadcast_to(jnp.sum(ind[s].astype(F32), axis=0, keepdims=True), (8, CL))
        g = gb[s].reshape(256, D).astype(F32)
        sq = g * g
        hi = sq.astype(BF)
        lo = (sq - hi.astype(F32)).astype(BF)
        ones = jnp.ones((8, D), BF)
        nrow[s] = (nt_dot(ones, hi) + nt_dot(ones, lo)) * inv
        ncol[s] = jnp.broadcast_to(jnp.sum(sq, axis=1, keepdims=True) * inv, (256, CL))

    def tile(lrows, lnorm, s):
        g = gb[s].reshape(256, D)
        prod = nt_dot(lrows, g)
        norm = jnp.concatenate([lnorm, lnorm], axis=1)
        kern = jnp.exp(prod * (2.0 * inv) - (norm + nrow[s][0:1])).astype(BF)
        return jnp.dot(kern, ind[s], preferred_element_type=F32)

    def self_sums(s, t):
        sums = tile(gb[t].reshape(256, D), ncol[t], s)
        return jnp.sum(ind[t].astype(F32) * sums, axis=0, keepdims=True)

    for s in range(SETS + 3):
        if s < SETS:
            ring_step(s)
            select(s)
            dispatch(s)
            for b, m in ((0, zl - s), (1, zl + s + 1)):
                if s < ZL:
                    pl.when((m >= 0) & (m < ZL))(lambda b=b, m=m, s=s: row_sends(s, b, m))
        if 1 <= s <= SETS:
            x_step(s - 1)
        if 2 <= s <= SETS + 1:
            relay(s - 2)
        if s == 6:
            row_relay()
        if 3 <= s:
            x_done(s - 3)
    row_done()

    for t in range(ROWS // RT):
        rows = pl.ds(t * RT, RT)
        v = rowb[rows, :].astype(F32)
        nleft[rows, :] = jnp.broadcast_to(jnp.sum(v * v, axis=1, keepdims=True) * inv, (RT, CL))
    o_ref[...] = jnp.zeros_like(o_ref)
    self_acc[...] = jnp.zeros_like(self_acc)
    cnt_acc[...] = jnp.zeros_like(cnt_acc)

    def per_set(s, carry):
        prepare(s)

        def per_rows(t, carry):
            rows = pl.ds(pl.multiple_of(t * RT, RT), RT)
            o_ref[rows, :] += tile(rowb[rows, :], nleft[rows, :], s)
            return carry

        lax.fori_loop(0, ROWS // RT, per_rows, 0)
        total = lax.fori_loop(0, s, lambda t, acc: acc + 2.0 * self_sums(s, t), self_sums(s, s))
        self_acc[...] += jnp.broadcast_to(total, (8, CL))
        return carry

    lax.fori_loop(0, SETS, per_set, 0)

    m_inv = 1.0 / jnp.maximum(cnt_acc[0:1], 1.0)
    base = 1.0 + self_acc[0:1] * (m_inv * m_inv)
    slope = 2.0 * m_inv

    def finish(t, carry):
        rows = pl.ds(pl.multiple_of(t * RT, RT), RT)
        o_ref[rows, :] = base - slope * o_ref[rows, :]
        return carry

    lax.fori_loop(0, ROWS // RT, finish, 0)

    for cp in pending:
        cp.wait_send()
    for m in range(ZL):
        for dy in range(NY):
            dst = row_at(0, m, k)
            pltpu.make_async_remote_copy(dst, dst, rsend_sem.at[dy, m], rr_sem.at[dy, m],
                                         device_id=partner, device_id_type=MESH).wait_send()


def per_device(points, assign):
    dma = pltpu.SemaphoreType.DMA
    vmem = pltpu.VMEM
    return pl.pallas_call(
        kernel,
        out_shape=jax.ShapeDtypeStruct((ROWS, CL), F32),
        in_specs=[pl.BlockSpec(memory_space=pltpu.VMEM)] * 2,
        out_specs=pl.BlockSpec(memory_space=pltpu.VMEM),
        scratch_shapes=[
            vmem((SETS, 2, PD, D), BF),
            vmem((SETS, 2, 8, 2 * PD), BF),
            vmem((SETS, PD, D), BF),
            vmem((SETS, PD, CL), BF),
            vmem((SETS, NX, PD, D), BF),
            vmem((SETS, CL, CL), BF),
            vmem((SETS, NX, 8, CL), F32),
            vmem((ROWS, D), BF),
            vmem((SETS, 256, CL), BF),
            vmem((SETS, 8, 256), F32),
            vmem((SETS, 256, CL), F32),
            vmem((ROWS, CL), F32),
            vmem((8, CL), F32),
            vmem((8, CL), F32),
            dma((SETS, 2, 2)),
            dma((SETS, 2)),
            dma((SETS,)),
            dma((SETS,)),
            dma((SETS, 2)),
            dma((SETS, 2)),
            dma((SETS, 3)),
            dma((NY, ZL)),
            dma((NY, ZL)),
            dma((320,)),
            dma((NY, ZL)),
        ],
        compiler_params=pltpu.CompilerParams(
            collective_id=0, has_side_effects=True, vmem_limit_bytes=60 * 1024 * 1024
        ),
        name="kmeans",
    )(points, assign.reshape(1, PD))


def solution(mesh):
    return jax.shard_map(
        per_device,
        mesh=mesh,
        in_specs=(P(("row", "col"), None), P(("row", "col"))),
        out_specs=P("row", "col"),
        check_vma=False,
    )
```

time: 274 us -> 112 us (0.41)
  the two profiles are of different devices: /device:TPU:8 before, /device:TPU:1 now
where the time goes in v1:
time: 112 us; the launch traced here: 111 us
  Pallas kernels  109 us (97%)
  local copies, waits for them, and re-layouts  2.26 us (2%)
    pallas_call x1, Pallas kernels, per_device(): pl.pallas_call(kernel, out_shape=jax.ShapeDtypeStruct((ROWS, CL), F32), i...  109 us
    unnamed x1, local copies, waits for them, and re-layouts  2.26 us

profile of v1, /device:TPU:1, one launch (start us, length us, event | category | flops | bytes accessed | tf_op | source)
XLA Modules:
  0.0 111.1 jit_solution(10252524343427764804)
XLA Ops:
  0.0 108.8 %kmeans.1 = f32[2048,128]{1,0:T(8,128)} custom-call(bf16[64,768]{1,0:T(8,128)(2,1)} %p_ref.1, s32[1,64]{1,0:T(1,128)} %bitcast.1), custom_call_target="tpu_custom_call" | custom-call | tf_op jit(solution)/shard_map/kmeans/pallas_call | solution.py:304
  108.8 2.3 %copy.4 = f32[2048,128]{1,0:T(8,128)} copy(f32[2048,128]{1,0:T(8,128)} %kmeans.1) | data formatting | bytes 2097152

commit v2 on v1

v2 whole, which is shorter than its diff:
```python
import jax
import jax.numpy as jnp
from jax import lax
from jax.experimental import pallas as pl
from jax.experimental.pallas import tpu as pltpu
from jax.sharding import PartitionSpec as P

D = 768
CL = 128
PD = 64
SLOT = 4
NX, NY, NZ, ZL = 4, 4, 16, 4
SETS = 8
ROWS = 2048
CHUNKS = 4
PAIR = 512
MESH = pl.DeviceIdType.MESH
F32 = jnp.float32
BF = jnp.bfloat16


def iota(shape, dim):
    return lax.broadcasted_iota(jnp.int32, shape, dim)


def nt_dot(left, right):
    return lax.dot_general(left, right, (((1,), (1,)), ((), ())), preferred_element_type=F32)


def kernel(p_ref, a_ref, o_ref, zb, zm, seld, selo, gb, yo, ids, rowb, ind, nrow, nown, nleft,
           self_acc, cnt_acc, part, zr_sem, zmr_sem, yd_sem, yo_sem, x_sem, xl_sem, id_sem,
           rr_sem, rp_sem, part_sem, send_sem, rsend_sem, psend_sem):
    r = lax.axis_index("row")
    c = lax.axis_index("col")
    x = lax.rem(r, NX)
    zh = r // NX
    y = c // (2 * ZL)
    zl = lax.rem(c // 2, ZL)
    k = lax.rem(c, 2)
    z = zh * ZL + zl

    def dev(dx, dy, dz, other):
        nx = lax.rem(x + dx, NX)
        ny = lax.rem(y + dy, NY)
        nz = lax.rem(z + dz, NZ)
        nk = 1 - k if other is True else (k if other is False else other)
        return (nz // ZL * NX + nx, (ny * ZL + lax.rem(nz, ZL)) * 2 + nk)

    inv = 1.0 / D
    right, left = dev(0, 0, 1, False), dev(0, 0, NZ - 1, False)
    partner = dev(0, 0, 0, True)
    pending = []
    count = [0]

    def send(src, dst, recv, device):
        sem = send_sem.at[count[0]]
        count[0] += 1
        cp = pltpu.make_async_remote_copy(src, dst, sem, recv, device_id=device, device_id_type=MESH)
        cp.start()
        pending.append(cp)

    def arrived(dst, recv):
        pltpu.make_async_copy(dst, dst, recv).wait()

    yo[...] = jnp.zeros_like(yo)
    self_acc[...] = jnp.zeros_like(self_acc)
    cnt_acc[...] = jnp.zeros_like(cnt_acc)
    barrier = pltpu.get_barrier_semaphore()
    peers = [right, left, partner]
    for dy in (1, 2, 3):
        peers += [dev(0, dy, 0, False), dev(0, dy, 0, True)]
    peers += [dev(dx, 0, 0, False) for dx in (1, 2, 3)]
    for peer in peers:
        pl.semaphore_signal(barrier, inc=1, device_id=peer, device_id_type=MESH)

    arow = a_ref[...]
    diag = iota((PD, PD), 0) == iota((PD, PD), 1)

    def to_col(row):
        return jnp.sum(jnp.where(diag, jnp.broadcast_to(row, (PD, PD)), 0), axis=1, keepdims=True)

    grow = arow // CL
    lrow = arow - grow * CL
    gcol = to_col(grow)
    earlier = (gcol == grow) & (iota((PD, PD), 0) < iota((PD, PD), 1))
    pos = jnp.sum(earlier.astype(jnp.int32), axis=0, keepdims=True)
    target = (grow * SLOT + pos).astype(F32)
    both = jnp.concatenate([target, lrow.astype(F32)], axis=1)
    zm[0, 0] = jnp.broadcast_to(both, (8, 2 * PD)).astype(BF)
    pl.semaphore_wait(barrier, len(peers))

    H = PD // 2
    Q = PD // CHUNKS

    def blk(s, b):
        return p_ref if (s, b) == (0, 0) else zb.at[s, b]

    def ring(s, b, half, ns, nb, device):
        send(blk(s, b).at[pl.ds(half * Q, Q)], zb.at[ns, nb, pl.ds(half * Q, Q)],
             zr_sem.at[ns, nb, half], device)

    def ring_meta(s, b, ns, nb, device):
        send(zm.at[s, b], zm.at[ns, nb], zmr_sem.at[ns, nb], device)

    nearest = ((0, 1, 2, 3), (0, 1, -1, 2), (0, 1, -1, -2), (0, -1, -2, -3))

    def by_zl(fn):
        for v in range(ZL):
            pl.when(zl == v)(lambda v=v: fn(v))

    def row_sends(i, dys):
        def go(v):
            d = nearest[v][i]
            m = v + d
            src = blk(-d, 0) if d <= 0 else blk(d - 1, 1)
            dst = row_at(0, m, k)
            for dy in dys:
                if dy == 0:
                    pltpu.make_async_copy(src, dst, rr_sem.at[0, m]).start()
                    pltpu.make_async_remote_copy(src, dst, rsend_sem.at[0, m], rp_sem.at[0, m],
                                                 device_id=partner, device_id_type=MESH).start()
                else:
                    pltpu.make_async_remote_copy(src, dst, rsend_sem.at[dy, m], rr_sem.at[dy, m],
                                                 device_id=dev(0, dy, 0, False),
                                                 device_id_type=MESH).start()
        by_zl(go)

    def row_pass(i, dys):
        def go(v):
            m = v + nearest[v][i]
            for dy in dys:
                ref = row_at(dy, m, k)
                arrived(ref, rr_sem.at[dy, m])
                pltpu.make_async_remote_copy(ref, ref, psend_sem.at[dy, m], rp_sem.at[dy, m],
                                             device_id=partner, device_id_type=MESH).start()
        by_zl(go)

    def row_at(dy, m, core):
        ys = lax.rem(y + NY - dy, NY)
        return rowb.at[pl.ds(pl.multiple_of(((ys * ZL + m) * 2 + core) * PD, PD), PD)]

    for half in range(CHUNKS):
        ring(0, 0, half, 1, 0, right)
        ring(0, 0, half, 0, 1, left)
        if half == 0:
            ring_meta(0, 0, 1, 0, right)
            ring_meta(0, 0, 0, 1, left)

    def ring_step(s):
        for half in range(CHUNKS):
            arrived(zb.at[s, 1, pl.ds(half * Q, Q)], zr_sem.at[s, 1, half])
            if s < SETS - 1:
                ring(s, 1, half, s + 1, 1, left)
            if s > 0:
                arrived(zb.at[s, 0, pl.ds(half * Q, Q)], zr_sem.at[s, 0, half])
                if s < SETS - 1:
                    ring(s, 0, half, s + 1, 0, right)
            if half == 0:
                arrived(zm.at[s, 1], zmr_sem.at[s, 1])
                if s < SETS - 1:
                    ring_meta(s, 1, s + 1, 1, left)
                if s > 0:
                    arrived(zm.at[s, 0], zmr_sem.at[s, 0])
                    if s < SETS - 1:
                        ring_meta(s, 0, s + 1, 0, right)

    def select(s):
        q = iota((PD, PD), 0)
        dy, core, b, p = q // 16, q // 8 % 2, q // 4 % 2, q % 4
        want = ((lax.rem(y + dy, NY) * ZL + zl) * 2 + core) * SLOT + p
        data = jnp.zeros((PD, D), F32)
        hot = jnp.zeros((PD, CL), F32)
        for bb in (0, 1):
            meta = zm[s, bb][0:1].astype(F32).astype(jnp.int32)
            trow, lrow_ = meta[:, :PD], meta[:, PD:]
            pick = ((trow == want) & (b == bb)).astype(BF)
            local = (to_col(lrow_) == iota((PD, CL), 1)).astype(BF)
            data += jnp.dot(pick, blk(s, bb)[...], preferred_element_type=F32)
            hot += jnp.dot(pick, local, preferred_element_type=F32)
        seld[s] = data.astype(BF)
        selo[s] = hot.astype(BF)

    def dispatch(s):
        for dy in (1, 3, 2, 0):
            src = ((NY - dy) % NY * 2 + k) * 8
            for core in (0, 1):
                if dy == 0 and core == 1:
                    continue
                at = dy * 16 + core * 8
                if dy == 0:
                    dest = partner
                    off = pl.multiple_of((1 - k) * 8, 8)
                else:
                    dest = dev(0, dy, 0, core)
                    off = at
                to = pl.ds(pl.multiple_of(src, 8), 8)
                send(seld.at[s, pl.ds(off, 8)], gb.at[s, 0, to], yd_sem.at[s], dest)
                send(selo.at[s, pl.ds(off, 8)], yo.at[s, to], yo_sem.at[s], dest)
        off = pl.ds(pl.multiple_of(k * 8, 8), 8)
        pltpu.make_async_copy(seld.at[s, off], gb.at[s, 0, off], yd_sem.at[s]).start()
        pltpu.make_async_copy(selo.at[s, off], yo.at[s, off], yo_sem.at[s]).start()

    def x_step(s):
        arrived(gb.at[s, 0], yd_sem.at[s])
        arrived(yo.at[s, pl.ds(0, PD)], yo_sem.at[s])
        send(gb.at[s, 0], gb.at[s, 3], x_sem.at[s, 0], dev(1, 0, 0, False))
        send(gb.at[s, 0], gb.at[s, 1], x_sem.at[s, 1], dev(3, 0, 0, False))
        number = (iota((8, CL), 1) + 1).astype(F32).astype(BF)
        v = gb[s, 0].astype(F32)
        sq = v * v
        hi = sq.astype(BF)
        lo = (sq - hi.astype(F32)).astype(BF)
        pad = jnp.zeros((PD, D), BF)
        ones = jnp.ones((8, D), BF)
        norm = nt_dot(ones, jnp.concatenate([hi, pad], axis=0)) + nt_dot(ones, jnp.concatenate([lo, pad], axis=0))
        ids[s, 0] = jnp.where(iota((8, CL), 0) == 0, nt_dot(number, yo[s]), norm * inv)
        nown[pl.ds(s * PD, PD), :] = jnp.broadcast_to(jnp.sum(sq, axis=1, keepdims=True) * inv, (PD, CL))
        for dx in (1, 2, 3):
            send(ids.at[s, 0], ids.at[s, NX - dx], id_sem.at[s, dx - 1], dev(dx, 0, 0, False))

    def relay(s):
        lo, hi = pl.ds(0, H), pl.ds(H, H)
        arrived(gb.at[s, 3], x_sem.at[s, 0])
        send(gb.at[s, 3, lo], gb.at[s, 2, lo], xl_sem.at[s, 0], dev(1, 0, 0, False))
        arrived(gb.at[s, 1], x_sem.at[s, 1])
        send(gb.at[s, 1, hi], gb.at[s, 2, hi], xl_sem.at[s, 1], dev(3, 0, 0, False))

    def x_done(s):
        arrived(gb.at[s, 2, pl.ds(0, H)], xl_sem.at[s, 0])
        arrived(gb.at[s, 2, pl.ds(H, H)], xl_sem.at[s, 1])
        for dx in (1, 2, 3):
            arrived(ids.at[s, NX - dx], id_sem.at[s, dx - 1])

    def tile_ready(dy):
        if dy == 0:
            for m in range(ZL):
                arrived(row_at(0, m, k), rr_sem.at[0, m])
        for m in range(ZL):
            arrived(row_at(dy, m, 1 - k), rp_sem.at[dy, m])
        rows = tile_rows(dy)
        v = rowb[rows, :].astype(F32)
        nleft[rows, :] = jnp.broadcast_to(jnp.sum(v * v, axis=1, keepdims=True) * inv, (PAIR, CL))

    def tile_rows(dy):
        return pl.ds(pl.multiple_of(lax.rem(y + NY - dy, NY) * PAIR, PAIR), PAIR)

    def prepare(s):
        def wide(row):
            ab = ids[s, 0, row:row + 1] + pltpu.roll(ids[s, 1, row:row + 1], PD, 1)
            cd = ids[s, 2, row:row + 1] + pltpu.roll(ids[s, 3, row:row + 1], PD, 1)
            return jnp.concatenate([ab, cd], axis=1)
        number = wide(0)
        hot = (number.astype(jnp.int32) - 1 == iota((CL, 256), 0)).astype(F32)
        ind[s] = hot.T.astype(BF)
        cnt_acc[...] += jnp.broadcast_to(jnp.sum(hot.T, axis=0, keepdims=True), (8, CL))
        nrow[s] = jnp.broadcast_to(wide(1), (8, 256))

    def tile(lrows, lnorm, s, n):
        g = gb[pl.ds(s, n)].reshape(n * 256, D)
        prod = nt_dot(lrows, g)
        right = jnp.concatenate([nrow[s + i][0:1] for i in range(n)], axis=1)
        norm = jnp.concatenate([lnorm] * (2 * n), axis=1)
        kern = jnp.exp(prod * (2.0 * inv) - (norm + right)).astype(BF)
        return jnp.dot(kern, ind[pl.ds(s, n)].reshape(n * 256, CL), preferred_element_type=F32)

    def unit(dy, s, n=2):
        rows = tile_rows(dy)
        o_ref[rows, :] += tile(rowb[rows, :], nleft[rows, :], s, n)

    def self_unit(s, n=2):
        own = gb[:, 0].reshape(PAIR, D)
        sums = tile(own, nown[...], s, n)
        hot = yo[:, 0:PD].reshape(PAIR, CL).astype(F32)
        self_acc[...] += jnp.broadcast_to(jnp.sum(hot * sums, axis=0, keepdims=True), (8, CL))

    o_ref[...] = jnp.zeros_like(o_ref)
    for s in range(SETS):
        ring_step(s)
        select(s)
        dispatch(s)
        if s < 4:
            row_sends(s, (0, 1, 3))
        if s >= 1:
            x_step(s - 1)
        if 3 <= s <= 6:
            row_sends(s - 3, (2,))
        if 2 <= s <= 5:
            row_pass(s - 2, (1, 3))
        if s == 4:
            tile_ready(0)
        if s == 6:
            tile_ready(1)
            tile_ready(3)
        if s >= 4:
            x_done(s - 4)
            prepare(s - 4)
        if s == 5:
            unit(0, 0)
        if s == 6:
            unit(1, 0)
        if s == 7:
            unit(3, 0)
        if s >= 2:
            relay(s - 2)

    relay(6)
    for i in range(4):
        row_pass(i, (2,))
    x_step(7)
    unit(0, 2)
    tile_ready(2)
    unit(2, 0)
    lax.fori_loop(1, 4, lambda i, carry: (unit(i, 2), carry)[1], 0)
    relay(7)
    for s in (4, 5):
        x_done(s)
        prepare(s)
    lax.fori_loop(0, 4, lambda i, carry: (unit(i, 4), carry)[1], 0)
    lax.fori_loop(0, 3, lambda i, carry: (self_unit(2 * i), carry)[1], 0)
    for s in (6, 7):
        x_done(s)
        prepare(s)
    self_unit(6)
    part[0] = self_acc[...]
    for dx in (1, 2, 3):
        send(part.at[0], part.at[NX - dx], part_sem.at[dx - 1], dev(dx, 0, 0, False))
    lax.fori_loop(0, 4, lambda i, carry: (unit(i, 6), carry)[1], 0)
    for dx in (1, 2, 3):
        arrived(part.at[NX - dx], part_sem.at[dx - 1])
    total = part[0] + part[1] + part[2] + part[3]

    m_inv = 1.0 / jnp.maximum(cnt_acc[0:1], 1.0)
    base = 1.0 + total[0:1] * (m_inv * m_inv)
    slope = 2.0 * m_inv

    def finish(t, carry):
        rows = pl.ds(pl.multiple_of(t * PAIR, PAIR), PAIR)
        o_ref[rows, :] = base - slope * o_ref[rows, :]
        return carry

    lax.fori_loop(0, ROWS // PAIR, finish, 0)

    for cp in pending:
        cp.wait_send()
    for m in range(ZL):
        dst = row_at(0, m, k)
        for dy in range(NY):
            sems = (rsend_sem,) if dy == 0 else (rsend_sem, psend_sem)
            for sem in sems:
                pltpu.make_async_remote_copy(dst, dst, sem.at[dy, m], rr_sem.at[dy, m],
                                             device_id=partner, device_id_type=MESH).wait_send()


def per_device(points, assign):
    dma = pltpu.SemaphoreType.DMA
    vmem = pltpu.VMEM
    return pl.pallas_call(
        kernel,
        out_shape=jax.ShapeDtypeStruct((ROWS, CL), F32),
        in_specs=[pl.BlockSpec(memory_space=pltpu.VMEM)] * 2,
        out_specs=pl.BlockSpec(memory_space=pltpu.VMEM),
        scratch_shapes=[
            vmem((SETS, 2, PD, D), BF),
            vmem((SETS, 2, 8, 2 * PD), BF),
            vmem((SETS, PD, D), BF),
            vmem((SETS, PD, CL), BF),
            vmem((SETS, NX, PD, D), BF),
            vmem((SETS, CL, CL), BF),
            vmem((SETS, NX, 8, CL), F32),
            vmem((ROWS, D), BF),
            vmem((SETS, 256, CL), BF),
            vmem((SETS, 8, 256), F32),
            vmem((SETS * PD, CL), F32),
            vmem((ROWS, CL), F32),
            vmem((8, CL), F32),
            vmem((8, CL), F32),
            vmem((NX, 8, CL), F32),
            dma((SETS, 2, CHUNKS)),
            dma((SETS, 2)),
            dma((SETS,)),
            dma((SETS,)),
            dma((SETS, 2)),
            dma((SETS, 2)),
            dma((SETS, 3)),
            dma((NY, ZL)),
            dma((NY, ZL)),
            dma((3,)),
            dma((400,)),
            dma((NY, ZL)),
            dma((NY, ZL)),
        ],
        compiler_params=pltpu.CompilerParams(
            collective_id=0, has_side_effects=True, vmem_limit_bytes=28 * 1024 * 1024
        ),
        name="kmeans",
    )(points, assign.reshape(1, PD))


def solution(mesh):
    return jax.shard_map(
        per_device,
        mesh=mesh,
        in_specs=(P(("row", "col"), None), P(("row", "col"))),
        out_specs=P("row", "col"),
        check_vma=False,
    )
```

time: 112 us -> 75.5 us (0.67)
  Pallas kernels: 109 us -> 72.9 us
    pallas_call x1, Pallas kernels: 109 us -> 72.9 us  [per_device(): pl.pallas_call(kernel, out_shape=jax.ShapeDtypeStruct((ROWS, CL), F32), i...]
    unnamed x1 -> x5, local copies, waits for them, and re-layouts: 2.26 us -> 2.52 us
where the time goes in v2:
time: 75.5 us; the launch traced here: 75.4 us
  Pallas kernels  72.9 us (97%)
  local copies, waits for them, and re-layouts  2.52 us (3%)
    pallas_call x1, Pallas kernels, per_device(): pl.pallas_call(kernel, out_shape=jax.ShapeDtypeStruct((ROWS, CL), F32), i...  72.9 us
    unnamed x5, local copies, waits for them, and re-layouts  2.52 us

profile of v2, /device:TPU:1, one launch (start us, length us, event | category | flops | bytes accessed | tf_op | source)
XLA Modules:
  0.0 75.4 jit_solution(9590023149293309978)
XLA Ops:
  0.0 0.0 copy-start.1
  0.0 0.7 copy-done.1
  0.7 0.0 copy-start
  0.7 0.9 %copy-done = bf16[64,768]{1,0:T(8,128)(2,1)S(1)} copy-done((bf16[64,768]{1,0:T(8,128)(2,1)S(1)}, bf16[64,768]{1,0:T(8,128)(2,1)}, u32[]{:S(2)}) %copy-start) | copy-done | bytes 98328
  1.5 72.9 %kmeans.1 = f32[2048,128]{1,0:T(8,128)S(1)} custom-call(bf16[64,768]{1,0:T(8,128)(2,1)S(1)} %copy-done, s32[1,64]{1,0:T(1,128)S(1)} %bitcast.1), custom_call_target="tpu_custom_call" | custom-call | tf_op jit(solution)/shard_map/kmeans/pallas_call | solution.py:357
  74.4 1.0 %copy.4 = f32[2048,128]{1,0:T(8,128)} copy(f32[2048,128]{1,0:T(8,128)S(1)} %kmeans.1) | data formatting | bytes 2097152
Async XLA Ops:
  0.0 0.7 copy-start.1
  0.7 0.9 %copy-start = (bf16[64,768]{1,0:T(8,128)(2,1)S(1)}, bf16[64,768]{1,0:T(8,128)(2,1)}, u32[]{:S(2)}) copy-start(bf16[64,768]{1,0:T(8,128)(2,1)} %p_ref.1) | copy-start | bytes 294916
